TPU v7x, 512 devices: a whole 4x4x16 slice. The times are simulated.
512 devices in a mesh: row: 32 (over z, y_lo), col: 16 (over y_hi, x, core).
Axes of the slice: x: 4, y: 4 (y_hi: 2, y_lo: 2; y = y_hi * 2 + y_lo), z: 16, core: 2. Of those that a mesh axis runs over, the one named last changes fastest.
Arguments:
- atom_feats: bfloat16 [32768, 128], P(('row', 'col')), may hold values from -6 to 6
- key_starts: int32 [1024], P(('row', 'col')), may hold values from -64 to 32704, as said below
- atom_counts: int32 [2048], replicated, may hold values from 8 to 24, as said below
- atom_gain: float32 [128], replicated, may hold values from 0.1 to 1.9
- w_query: bfloat16 [128, 128], replicated, may hold values from -0.5 to 0.5
- w_key: bfloat16 [128, 128], replicated, may hold values from -0.5 to 0.5
- w_value: bfloat16 [128, 128], replicated, may hold values from -0.5 to 0.5
- w_out: bfloat16 [128, 128], replicated, may hold values from -0.5 to 0.5
- w_pool: bfloat16 [128, 384], replicated, may hold values from -0.5 to 0.5
- w_back: bfloat16 [384, 128], replicated, may hold values from -0.3125 to 0.3125
- pair_state: bfloat16 [2048, 2048, 128], P('row', 'col'), may hold values from -6 to 6
- w_left: bfloat16 [384, 32], replicated, may hold values from -0.3125 to 0.3125
- w_right: bfloat16 [384, 32], replicated, may hold values from -0.3125 to 0.3125
- w_outer: bfloat16 [32, 32, 128], replicated, may hold values from -0.1875 to 0.1875
- pair_gain: float32 [128], replicated, may hold values from 0.1 to 1.9
- w_gate: bfloat16 [128, 512], replicated, may hold values from -0.5 to 0.5
- w_lift: bfloat16 [128, 512], replicated, may hold values from -0.5 to 0.5
- w_drop: bfloat16 [512, 128], replicated, may hold values from -0.25 to 0.25
Outputs:
- atom_out: bfloat16 [32768, 128], P(('row', 'col'))
- token_single: bfloat16 [2048, 384], P(('row', 'col'))
- pair_out: bfloat16 [2048, 2048, 128], P('row', 'col')
Inputs may be any that keep to these rules, and one draw needn't show every extreme that they name: key_starts[b] = 32 * b - 64 + offset, with offset a whole number from 0 to 32; the offset is 0 for the first block and 32 for the last. `atom_counts`: the counts sum to 32768.
All inputs are finite; a program needn't handle non-finite values.
Results may differ from a plain program's by a relative error of at most 0.007.
Values may be sent and summed in bfloat16 or wider, within the bound.
A program may use at most 64 MiB of HBM per device.

v0:
```python
import math
import jax
import jax.numpy as jnp
from jax import lax
from jax.sharding import PartitionSpec as P

HEADS = 4
QB = 32
KW = 128
FEWEST = 8
EPSILON = 1e-05


def with_halo(block, sides, width):
    for axis, dim in sides:
        count = lax.axis_size(axis)
        forward = [(i, i + 1) for i in range(count - 1)]
        backward = [(target, source) for source, target in forward]
        low = lax.ppermute(
            lax.slice_in_dim(block, block.shape[dim] - width, None, axis=dim), axis, forward
        )
        high = lax.ppermute(lax.slice_in_dim(block, 0, width, axis=dim), axis, backward)
        block = jnp.concatenate([low, block, high], axis=dim)
    return block


def shifted(block, axis, distance):
    devices = range(lax.axis_size(axis))
    route = [(i - distance, i) for i in devices if i - distance in devices]
    return lax.ppermute(block, axis, route)


def layer_norm(values, gain):
    mean_value = jnp.mean(values, axis=-1, keepdims=True)
    centred = values - mean_value
    variance = jnp.mean(centred * centred, axis=-1, keepdims=True)
    return centred * lax.rsqrt(variance + EPSILON) * gain


def project(source, weight):
    return jnp.dot(source, weight, preferred_element_type=jnp.float32).astype(jnp.bfloat16)


def per_device(
    atom_feats,
    key_starts,
    atom_counts,
    atom_gain,
    w_query,
    w_key,
    w_value,
    w_out,
    w_pool,
    w_back,
    pair_state,
    w_left,
    w_right,
    w_outer,
    pair_gain,
    w_gate,
    w_lift,
    w_drop,
):
    atom_rows, atom_width = atom_feats.shape
    devices = lax.axis_size(("row", "col"))
    position = lax.axis_index(("row", "col"))
    total_atoms = atom_rows * devices
    total_tokens = atom_counts.shape[0]
    own_tokens = total_tokens // devices
    rim_width = KW // 2
    first_atom = position * atom_rows
    atom_float = atom_feats.astype(jnp.float32)
    normed = layer_norm(atom_float, atom_gain).astype(jnp.bfloat16)
    queries = project(normed, w_query)
    w_keyval = jnp.concatenate([w_key, w_value], axis=1)
    keyvals = project(normed, w_keyval)
    extended = with_halo(keyvals, ((("row", "col"), 0),), rim_width)
    local_starts = key_starts - first_atom + rim_width
    windows = jax.vmap(lambda first_row: lax.dynamic_slice_in_dim(extended, first_row, KW, 0))(
        local_starts
    )
    head_size = atom_width // HEADS
    blocks = atom_rows // QB
    query_blocks = queries.reshape(blocks, QB, HEADS, head_size)
    key_blocks = windows[:, :, :atom_width].reshape(blocks, KW, HEADS, head_size)
    value_blocks = windows[:, :, atom_width:].reshape(blocks, KW, HEADS, head_size)
    key_index = key_starts[:, None] + jnp.arange(KW, dtype=jnp.int32)[None, :]
    in_range = (key_index >= 0) & (key_index < total_atoms)
    scores = jnp.einsum(
        "bqhd,bkhd->bhqk", query_blocks, key_blocks, preferred_element_type=jnp.float32
    ) * head_size ** (-0.5)
    raised = jnp.where(in_range[:, None, None, :], jnp.exp(scores), 0.0)
    weights = (raised / jnp.sum(raised, axis=-1, keepdims=True)).astype(jnp.bfloat16)
    attended = (
        jnp.einsum("bhqk,bkhd->bqhd", weights, value_blocks, preferred_element_type=jnp.float32)
        .astype(jnp.bfloat16)
        .reshape(atom_rows, atom_width)
    )
    updated = (atom_float + jnp.dot(attended, w_out, preferred_element_type=jnp.float32)).astype(
        jnp.bfloat16
    )
    feature = jax.nn.relu(jnp.dot(updated, w_pool, preferred_element_type=jnp.float32)).astype(
        jnp.bfloat16
    )
    token_ends = jnp.cumsum(atom_counts, dtype=jnp.int32)
    atom_index = first_atom + jnp.arange(atom_rows, dtype=jnp.int32)
    token_of = jnp.sum((token_ends[None, :] <= atom_index[:, None]).astype(jnp.int32), axis=1)
    count_float = atom_counts.astype(jnp.float32)
    slots = atom_rows // FEWEST
    token_starts = token_ends - atom_counts
    base_token = jnp.sum((token_starts < first_atom).astype(jnp.int32))
    relative = token_of - base_token
    slot_range = jnp.arange(slots, dtype=jnp.int32)
    member = (relative[:, None] == slot_range[None, :]).astype(jnp.bfloat16)
    local_sums = jnp.einsum("as,ac->sc", member, feature, preferred_element_type=jnp.float32)
    carried = (relative < 0).astype(jnp.bfloat16)[None, :]
    edge_sum = jnp.dot(carried, feature, preferred_element_type=jnp.float32)
    from_next = shifted(edge_sum, ("row", "col"), -1)
    next_token = jnp.sum((token_ends <= first_atom + atom_rows).astype(jnp.int32))
    target = (slot_range == next_token - base_token).astype(jnp.float32)[:, None]
    pooled_slots = local_sums + target * from_next
    padded_counts = jnp.concatenate([count_float, jnp.ones((slots,), jnp.float32)])
    slot_counts = lax.dynamic_slice_in_dim(padded_counts, base_token, slots, 0)
    slot_single = (pooled_slots / slot_counts[:, None]).astype(jnp.bfloat16)
    owner = token_starts // atom_rows
    owner_first = jnp.searchsorted(token_starts, owner * atom_rows, side="left")
    row_of = owner * slots + jnp.arange(total_tokens, dtype=jnp.int32) - owner_first
    gathered = lax.all_gather(slot_single, ("row", "col"), axis=0, tiled=True)
    full_single = jnp.take(gathered, row_of, axis=0)
    left_all = project(full_single, w_left)
    right_all = project(full_single, w_right)
    back_all = project(full_single, w_back)
    token_single = lax.dynamic_slice_in_dim(full_single, position * own_tokens, own_tokens, 0)
    member_all = (token_of[:, None] == jnp.arange(total_tokens, dtype=jnp.int32)[None, :]).astype(
        jnp.bfloat16
    )
    lifted = jnp.dot(member_all, back_all, preferred_element_type=jnp.float32)
    atom_out = (updated.astype(jnp.float32) + lifted).astype(jnp.bfloat16)
    row_tokens, col_tokens, pair_width = pair_state.shape
    left_rows = lax.dynamic_slice_in_dim(
        left_all, lax.axis_index("row") * row_tokens, row_tokens, 0
    )
    right_cols = lax.dynamic_slice_in_dim(
        right_all, lax.axis_index("col") * col_tokens, col_tokens, 0
    )
    outer_table = jnp.einsum(
        "jb,abc->jac", right_cols, w_outer, preferred_element_type=jnp.float32
    ).astype(jnp.bfloat16)
    step_rows = math.gcd(row_tokens, 8)

    def pair_block(pieces):
        left_block, pair_piece = pieces
        outer_term = jnp.einsum(
            "ia,jac->ijc", left_block, outer_table, preferred_element_type=jnp.float32
        )
        summed = pair_piece.astype(jnp.float32) + outer_term
        normed_pair = layer_norm(summed, pair_gain).astype(jnp.bfloat16)
        gate_proj = jnp.einsum(
            "ijc,cf->ijf", normed_pair, w_gate, preferred_element_type=jnp.float32
        )
        lift_proj = jnp.einsum(
            "ijc,cf->ijf", normed_pair, w_lift, preferred_element_type=jnp.float32
        )
        hidden = (jax.nn.silu(gate_proj) * lift_proj).astype(jnp.bfloat16)
        return (
            summed + jnp.einsum("ijf,fc->ijc", hidden, w_drop, preferred_element_type=jnp.float32)
        ).astype(jnp.bfloat16)

    pair_out = lax.map(
        pair_block,
        (
            left_rows.reshape(-1, step_rows, left_rows.shape[1]),
            pair_state.reshape(-1, step_rows, col_tokens, pair_width),
        ),
    )
    return (atom_out, token_single, pair_out.reshape(row_tokens, col_tokens, pair_width))


def solution(mesh):
    in_specs = (
        P(("row", "col"), None),
        P(("row", "col")),
        P(),
        P(),
        P(),
        P(),
        P(),
        P(),
        P(),
        P(),
        P("row", "col", None),
        P(),
        P(),
        P(),
        P(),
        P(),
        P(),
        P(),
    )
    out_specs = (P(("row", "col"), None), P(("row", "col"), None), P("row", "col", None))
    return jax.shard_map(
        per_device, mesh=mesh, in_specs=in_specs, out_specs=out_specs, check_vma=False
    )
```

profile of v0, /device:TPU:64, one launch (start us, length us, event | category | flops | bytes accessed | tf_op | source)
XLA Modules:
  0.0 1076.9 jit_solution(7566077309387999252)
XLA Ops:
  7.2 0.9 convert_reduce_fusion.1
  8.1 0.9 fusion.29
  9.0 1.0 convolution_convert_fusion.3
  10.0 6.1 collective-permute-start.1
  16.1 1.9 collective-permute-start
  18.1 0.7 compare_and_fusion.1
  18.8 0.7 fusion.42
  19.5 1.0 reduce-window.9
  20.7 0.9 broadcast_multiply_fusion.1
  21.5 0.7 convert_reduce_fusion.2
  22.2 1.0 convolution_convert_fusion.4
  23.2 142.4 %while.37 = (s32[]{:T(128)}, u32[2048]{0:T(1024)S(1)}, u32[2048]{0:T(1024)S(1)}, s32[2048]{0:T(1024)S(1)}, s32[2048]{0:T(1024)S(1)}, /*index=5*/s32[]{:T(128)}, s32[]{:T(128)}, s32[]{}) while((s32[]{:T(128)}, u32[2048]{0:T(1024)S(1)}, u32[2048]{0:T(1024)S(1)}, s32[2048]{0:T(1024)S(1)}, s32[2048]{0:T(1024)S(1)}, ...), condition=%wide.region_7.8_spmd.clone, body=%wide.region_6.7_spmd.clone.sunk | while | flops 38916 | bytes 135277 | solution.py:126
  23.2 11.8 %gather_fusion = s32[2048]{0:T(1024)S(1)} fusion(s32[2048]{0:T(1024)S(1)} %get-tuple-element.368, u32[2048]{0:T(1024)S(1)} %broadcast_clamp_fusion.3), kind=kCustom, calls=%fused_computation.clone.clone.1 | custom fusion | bytes 24576 | tf_op jit(solution)/shard_map/jit(searchsorted)/jit(_searchsorted_scan_impl)/vmap(jit(_searchsorted_scan_impl))/while/body/eval_jaxpr/gather | solution.py:126
  35.1 11.8 %gather_fusion = s32[2048]{0:T(1024)S(1)} fusion(s32[2048]{0:T(1024)S(1)} %get-tuple-element.368, u32[2048]{0:T(1024)S(1)} %broadcast_clamp_fusion.3), kind=kCustom, calls=%fused_computation.clone.clone.1 | custom fusion | bytes 24576 | tf_op jit(solution)/shard_map/jit(searchsorted)/jit(_searchsorted_scan_impl)/vmap(jit(_searchsorted_scan_impl))/while/body/eval_jaxpr/gather | solution.py:126
  47.0 11.8 %gather_fusion = s32[2048]{0:T(1024)S(1)} fusion(s32[2048]{0:T(1024)S(1)} %get-tuple-element.368, u32[2048]{0:T(1024)S(1)} %broadcast_clamp_fusion.3), kind=kCustom, calls=%fused_computation.clone.clone.1 | custom fusion | bytes 24576 | tf_op jit(solution)/shard_map/jit(searchsorted)/jit(_searchsorted_scan_impl)/vmap(jit(_searchsorted_scan_impl))/while/body/eval_jaxpr/gather | solution.py:126
  58.9 11.8 %gather_fusion = s32[2048]{0:T(1024)S(1)} fusion(s32[2048]{0:T(1024)S(1)} %get-tuple-element.368, u32[2048]{0:T(1024)S(1)} %broadcast_clamp_fusion.3), kind=kCustom, calls=%fused_computation.clone.clone.1 | custom fusion | bytes 24576 | tf_op jit(solution)/shard_map/jit(searchsorted)/jit(_searchsorted_scan_impl)/vmap(jit(_searchsorted_scan_impl))/while/body/eval_jaxpr/gather | solution.py:126
  70.7 11.8 %gather_fusion = s32[2048]{0:T(1024)S(1)} fusion(s32[2048]{0:T(1024)S(1)} %get-tuple-element.368, u32[2048]{0:T(1024)S(1)} %broadcast_clamp_fusion.3), kind=kCustom, calls=%fused_computation.clone.clone.1 | custom fusion | bytes 24576 | tf_op jit(solution)/shard_map/jit(searchsorted)/jit(_searchsorted_scan_impl)/vmap(jit(_searchsorted_scan_impl))/while/body/eval_jaxpr/gather | solution.py:126
  82.6 11.8 %gather_fusion = s32[2048]{0:T(1024)S(1)} fusion(s32[2048]{0:T(1024)S(1)} %get-tuple-element.368, u32[2048]{0:T(1024)S(1)} %broadcast_clamp_fusion.3), kind=kCustom, calls=%fused_computation.clone.clone.1 | custom fusion | bytes 24576 | tf_op jit(solution)/shard_map/jit(searchsorted)/jit(_searchsorted_scan_impl)/vmap(jit(_searchsorted_scan_impl))/while/body/eval_jaxpr/gather | solution.py:126
  94.5 11.8 %gather_fusion = s32[2048]{0:T(1024)S(1)} fusion(s32[2048]{0:T(1024)S(1)} %get-tuple-element.368, u32[2048]{0:T(1024)S(1)} %broadcast_clamp_fusion.3), kind=kCustom, calls=%fused_computation.clone.clone.1 | custom fusion | bytes 24576 | tf_op jit(solution)/shard_map/jit(searchsorted)/jit(_searchsorted_scan_impl)/vmap(jit(_searchsorted_scan_impl))/while/body/eval_jaxpr/gather | solution.py:126
  106.3 11.8 %gather_fusion = s32[2048]{0:T(1024)S(1)} fusion(s32[2048]{0:T(1024)S(1)} %get-tuple-element.368, u32[2048]{0:T(1024)S(1)} %broadcast_clamp_fusion.3), kind=kCustom, calls=%fused_computation.clone.clone.1 | custom fusion | bytes 24576 | tf_op jit(solution)/shard_map/jit(searchsorted)/jit(_searchsorted_scan_impl)/vmap(jit(_searchsorted_scan_impl))/while/body/eval_jaxpr/gather | solution.py:126
  118.2 11.8 %gather_fusion = s32[2048]{0:T(1024)S(1)} fusion(s32[2048]{0:T(1024)S(1)} %get-tuple-element.368, u32[2048]{0:T(1024)S(1)} %broadcast_clamp_fusion.3), kind=kCustom, calls=%fused_computation.clone.clone.1 | custom fusion | bytes 24576 | tf_op jit(solution)/shard_map/jit(searchsorted)/jit(_searchsorted_scan_impl)/vmap(jit(_searchsorted_scan_impl))/while/body/eval_jaxpr/gather | solution.py:126
  130.1 11.8 %gather_fusion = s32[2048]{0:T(1024)S(1)} fusion(s32[2048]{0:T(1024)S(1)} %get-tuple-element.368, u32[2048]{0:T(1024)S(1)} %broadcast_clamp_fusion.3), kind=kCustom, calls=%fused_computation.clone.clone.1 | custom fusion | bytes 24576 | tf_op jit(solution)/shard_map/jit(searchsorted)/jit(_searchsorted_scan_impl)/vmap(jit(_searchsorted_scan_impl))/while/body/eval_jaxpr/gather | solution.py:126
  141.9 11.8 %gather_fusion = s32[2048]{0:T(1024)S(1)} fusion(s32[2048]{0:T(1024)S(1)} %get-tuple-element.368, u32[2048]{0:T(1024)S(1)} %broadcast_clamp_fusion.3), kind=kCustom, calls=%fused_computation.clone.clone.1 | custom fusion | bytes 24576 | tf_op jit(solution)/shard_map/jit(searchsorted)/jit(_searchsorted_scan_impl)/vmap(jit(_searchsorted_scan_impl))/while/body/eval_jaxpr/gather | solution.py:126
  153.8 11.8 %gather_fusion = s32[2048]{0:T(1024)S(1)} fusion(s32[2048]{0:T(1024)S(1)} %get-tuple-element.368, u32[2048]{0:T(1024)S(1)} %broadcast_clamp_fusion.3), kind=kCustom, calls=%fused_computation.clone.clone.1 | custom fusion | bytes 24576 | tf_op jit(solution)/shard_map/jit(searchsorted)/jit(_searchsorted_scan_impl)/vmap(jit(_searchsorted_scan_impl))/while/body/eval_jaxpr/gather | solution.py:126
  172.2 7.9 collective-permute-start.2
  180.2 1.2 collective-permute-done.2
  181.4 0.8 divide_convert_fusion.2
  182.3 835.3 %all-gather.2.cloned.1.call-done = bf16[4096,384]{1,0:T(8,128)(2,1)} async-done(((bf16[8,384]{1,0:T(8,128)(2,1)}), bf16[4096,384]{1,0:T(8,128)(2,1)}) %all-gather.2.cloned.1.call-update) | async-done | bytes 3145744 | tf_op jit(solution)/shard_map/all_gather | solution.py:128
  1017.6 9.5 gather_fusion.1
  1028.0 1.4 fusion.19
  1031.8 0.7 copy.50
  1032.6 37.5 %while.35 = (s32[]{:T(128)}, bf16[8,8,128,128]{3,2,1,0:T(8,128)(2,1)}, bf16[8,8,128,128]{3,2,1,0:T(8,128)(2,1)}, bf16[8,8,32]{2,1,0:T(8,128)(2,1)S(1)}, bf16[128...) while((s32[]{:T(128)}, ...), condition=%wide.region_13.14_spmd, body=%wide.region_10.13_spmd.sunk | while | flops 415761408 | bytes 12229241 | solution.py:169
  1032.6 1.0 constant_dynamic-slice_fusion.5
  1035.1 0.7 multiply_convert_fusion.5
  1035.8 0.7 fusion.93
  1036.5 0.7 copy_dynamic-update-slice_fusion.2
  1037.3 1.0 constant_dynamic-slice_fusion.5
  1039.8 0.7 multiply_convert_fusion.5
  1040.5 0.7 fusion.93
  1041.2 0.7 copy_dynamic-update-slice_fusion.2
  1042.0 1.0 constant_dynamic-slice_fusion.5
  1044.5 0.7 multiply_convert_fusion.5
  1045.2 0.7 fusion.93
  1045.9 0.7 copy_dynamic-update-slice_fusion.2
  1046.7 1.0 constant_dynamic-slice_fusion.5
  1049.2 0.7 multiply_convert_fusion.5
  1049.9 0.7 fusion.93
  1050.6 0.7 copy_dynamic-update-slice_fusion.2
  1051.3 1.0 constant_dynamic-slice_fusion.5
  1053.8 0.7 multiply_convert_fusion.5
  1054.6 0.7 fusion.93
  1055.3 0.7 copy_dynamic-update-slice_fusion.2
  1056.0 1.0 constant_dynamic-slice_fusion.5
  1058.5 0.7 multiply_convert_fusion.5
  1059.2 0.7 fusion.93
  1060.0 0.7 copy_dynamic-update-slice_fusion.2
  1060.7 1.0 constant_dynamic-slice_fusion.5
  1063.2 0.7 multiply_convert_fusion.5
  1063.9 0.7 fusion.93
  1064.6 0.7 copy_dynamic-update-slice_fusion.2
  1065.4 1.0 constant_dynamic-slice_fusion.5
  1067.9 0.7 multiply_convert_fusion.5
  1068.6 0.7 fusion.93
  1069.3 0.7 copy_dynamic-update-slice_fusion.2
  (165 shorter events, 19.4 us)
Async XLA Ops:
  7.2 1024.2 %copy-start = (bf16[32,32,128]{2,1,0:T(8,128)(2,1)S(1)}, bf16[32,32,128]{2,1,0:T(8,128)(2,1)}, u32[]{:S(2)}) copy-start(bf16[32,32,128]{2,1,0:T(8,128)(2,1)} %param.35) | copy-start | bytes 786436
  7.2 1010.4 %all-gather.2.cloned.1.call-start = ((), (), s32[]{:S(2)}) async-start(), calls=%async_computation | async-start | bytes 3151872 | tf_op jit(solution)/shard_map/all_gather | solution.py:128
  10.0 160.6 %collective-permute-start.1 = (bf16[64,256]{1,0:T(8,128)(2,1)S(1)}, bf16[64,256]{1,0:T(8,128)(2,1)S(1)}, u32[]{:S(2)}, u32[]{:S(2)}) collective-permute-start(bf16[64,256]{1,0:T(8,128)(2,1)S(1)} %convolution_convert_fusion.3), channel_id=1, source_target_pairs={{1,0},{2,1},{3,2},{4,3},{5,4},{6,5},{7,6},{8,7},{9,8},{10,9},{11,1... | collective-permute-start | bytes 98312 | tf_op jit(solution)/shard_map/ppermute | solution.py:22
  16.1 154.5 %collective-permute-start = (bf16[64,256]{1,0:T(8,128)(2,1)S(1)}, bf16[64,256]{1,0:T(8,128)(2,1)S(1)}, u32[]{:S(2)}, u32[]{:S(2)}) collective-permute-start(bf16[64,256]{1,0:T(8,128)(2,1)S(1)} %convolution_convert_fusion.3), channel_id=1, source_target_pairs={{0,1},{1,2},{2,3},{3,4},{4,5},{5,6},{6,7},{7,8},{8,9},{9,10},{10,1... | collective-permute-start | bytes 98312 | tf_op jit(solution)/shard_map/ppermute | solution.py:19
  165.6 6.2 copy-start.3
  165.6 6.2 copy-start.5
  165.7 6.3 copy-start.4
  172.2 9.1 collective-permute-start.2
  1027.1 0.9 copy-start.10
  1027.1 2.9 copy-start.6
  1028.0 2.6 copy-start.7
  1031.1 1.4 copy-start.1
  1031.2 1.4 copy-start.2
  1031.2 1.4 copy-start.8
  1031.2 1.4 copy-start.9
Sparse Core Ops, SparseCore 0:
  182.4 835.1 all-gather.1
where the time goes:
time: 1080 us
  waiting for transfers between devices  836 us (77%)
  local copies, waits for them, and re-layouts  168 us (16%)
  matrix products  24.3 us (2%)
  between operations  17.7 us (2%)
  starting transfers between devices  15.9 us (1%)
  other arithmetic  13.9 us (1%)
    all_gather x1, waiting for transfers between devices, per_device(): gathered = lax.all_gather(slot_single, ('row', 'col'), axis=0, tiled=True)  835 us
    gather x12, local copies, waits for them, and re-layouts, per_device(): owner_first = jnp.searchsorted(token_starts, owner * atom_rows, side='left')  141 us
  transfers between devices with their start and end apart: 4, of which 2 were waited for; matrix products, arithmetic and copies ran while one was open for 14% of the time, Pallas kernels for 0%

commit v1 on v0

--- a/solution.py
+++ b/solution.py
@@ -125,7 +125,12 @@
     owner = token_starts // atom_rows
     owner_first = jnp.searchsorted(token_starts, owner * atom_rows, side="left")
     row_of = owner * slots + jnp.arange(total_tokens, dtype=jnp.int32) - owner_first
-    gathered = lax.all_gather(slot_single, ("row", "col"), axis=0, tiled=True)
+    gathered = jnp.concatenate(
+        lax.all_to_all(
+            jnp.stack([slot_single] * lax.axis_size(("row", "col"))), ("row", "col"), 0, 0
+        ),
+        axis=0,
+    )
     full_single = jnp.take(gathered, row_of, axis=0)
     left_all = project(full_single, w_left)
     right_all = project(full_single, w_right)

time: 1080 us -> 402 us (0.37)
  the two profiles are of different devices: /device:TPU:64 before, /device:TPU:1 now
where the time goes in v1:
time: 402 us
  local copies, waits for them, and re-layouts  169 us (42%)
  waiting for transfers between devices  149 us (37%)
  starting transfers between devices  40.8 us (10%)
  matrix products  22.9 us (6%)
  other arithmetic  15.1 us (4%)
  between operations  4.29 us (1%)
    all_to_all x1, waiting for transfers between devices, per_device(): lax.all_to_all(jnp.stack([slot_single] * lax.axis_size(('row', 'col'))),...  146 us
    gather x12, local copies, waits for them, and re-layouts, per_device(): owner_first = jnp.searchsorted(token_starts, owner * atom_rows, side='left')  141 us
    all_to_all x1, starting transfers between devices, per_device(): lax.all_to_all(jnp.stack([slot_single] * lax.axis_size(('row', 'col'))),...  27.7 us
    gather x1, local copies, waits for them, and re-layouts, per_device(): full_single = jnp.take(gathered, row_of, axis=0)  9.04 us
    ppermute x1, starting transfers between devices, with_halo(): lax.ppermute(lax.slice_in_dim(block, 0, width, axis=dim), axis, backward)  8.75 us
  transfers between devices with their start and end apart: 4, of which 2 were waited for; matrix products, arithmetic and copies ran while one was open for 37% of the time, Pallas kernels for 0%

profile of v1, /device:TPU:1, one launch (start us, length us, event | category | flops | bytes accessed | tf_op | source)
XLA Modules:
  0.0 401.6 jit_solution(13150332468949652769)
XLA Ops:
  0.6 0.9 convert_reduce_fusion.1
  1.5 0.9 fusion.29
  2.4 1.0 convolution_convert_fusion.3
  3.5 8.7 %collective-permute-start.1 = (bf16[64,256]{1,0:T(8,128)(2,1)S(1)}, bf16[64,256]{1,0:T(8,128)(2,1)S(1)}, u32[]{:S(2)}, u32[]{:S(2)}) collective-permute-start(bf16[64,256]{1,0:T(8,128)(2,1)S(1)} %convolution_convert_fusion.3), channel_id=1, source_target_pairs={{1,0},{2,1},{3,2},{4,3},{5,4},{6,5},{7,6},{8,7},{9,8},{10,9},{11,1... | collective-permute-start | bytes 98312 | tf_op jit(solution)/shard_map/ppermute | solution.py:22
  12.2 1.9 collective-permute-start
  14.2 0.7 compare_and_fusion.1
  15.6 1.0 reduce-window.9
  16.8 0.9 broadcast_multiply_fusion.1
  17.7 142.4 %while.37 = (s32[]{:T(128)}, u32[2048]{0:T(1024)S(1)}, u32[2048]{0:T(1024)S(1)}, s32[2048]{0:T(1024)S(1)}, s32[2048]{0:T(1024)S(1)}, /*index=5*/s32[]{:T(128)}, s32[]{:T(128)}, s32[]{}) while((s32[]{:T(128)}, u32[2048]{0:T(1024)S(1)}, u32[2048]{0:T(1024)S(1)}, s32[2048]{0:T(1024)S(1)}, s32[2048]{0:T(1024)S(1)}, ...), condition=%wide.region_7.8_spmd.clone, body=%wide.region_6.7_spmd.clone.sunk | while | flops 38916 | bytes 135285 | solution.py:126
  17.7 11.8 %gather_fusion = s32[2048]{0:T(1024)S(1)} fusion(s32[2048]{0:T(1024)S(1)} %get-tuple-element.368, u32[2048]{0:T(1024)S(1)} %broadcast_clamp_fusion.3), kind=kCustom, calls=%fused_computation.clone.clone.1 | custom fusion | bytes 24576 | tf_op jit(solution)/shard_map/jit(searchsorted)/jit(_searchsorted_scan_impl)/vmap(jit(_searchsorted_scan_impl))/while/body/eval_jaxpr/gather | solution.py:126
  29.6 11.8 %gather_fusion = s32[2048]{0:T(1024)S(1)} fusion(s32[2048]{0:T(1024)S(1)} %get-tuple-element.368, u32[2048]{0:T(1024)S(1)} %broadcast_clamp_fusion.3), kind=kCustom, calls=%fused_computation.clone.clone.1 | custom fusion | bytes 24576 | tf_op jit(solution)/shard_map/jit(searchsorted)/jit(_searchsorted_scan_impl)/vmap(jit(_searchsorted_scan_impl))/while/body/eval_jaxpr/gather | solution.py:126
  41.4 11.8 %gather_fusion = s32[2048]{0:T(1024)S(1)} fusion(s32[2048]{0:T(1024)S(1)} %get-tuple-element.368, u32[2048]{0:T(1024)S(1)} %broadcast_clamp_fusion.3), kind=kCustom, calls=%fused_computation.clone.clone.1 | custom fusion | bytes 24576 | tf_op jit(solution)/shard_map/jit(searchsorted)/jit(_searchsorted_scan_impl)/vmap(jit(_searchsorted_scan_impl))/while/body/eval_jaxpr/gather | solution.py:126
  53.3 11.8 %gather_fusion = s32[2048]{0:T(1024)S(1)} fusion(s32[2048]{0:T(1024)S(1)} %get-tuple-element.368, u32[2048]{0:T(1024)S(1)} %broadcast_clamp_fusion.3), kind=kCustom, calls=%fused_computation.clone.clone.1 | custom fusion | bytes 24576 | tf_op jit(solution)/shard_map/jit(searchsorted)/jit(_searchsorted_scan_impl)/vmap(jit(_searchsorted_scan_impl))/while/body/eval_jaxpr/gather | solution.py:126
  65.2 11.8 %gather_fusion = s32[2048]{0:T(1024)S(1)} fusion(s32[2048]{0:T(1024)S(1)} %get-tuple-element.368, u32[2048]{0:T(1024)S(1)} %broadcast_clamp_fusion.3), kind=kCustom, calls=%fused_computation.clone.clone.1 | custom fusion | bytes 24576 | tf_op jit(solution)/shard_map/jit(searchsorted)/jit(_searchsorted_scan_impl)/vmap(jit(_searchsorted_scan_impl))/while/body/eval_jaxpr/gather | solution.py:126
  77.0 11.8 %gather_fusion = s32[2048]{0:T(1024)S(1)} fusion(s32[2048]{0:T(1024)S(1)} %get-tuple-element.368, u32[2048]{0:T(1024)S(1)} %broadcast_clamp_fusion.3), kind=kCustom, calls=%fused_computation.clone.clone.1 | custom fusion | bytes 24576 | tf_op jit(solution)/shard_map/jit(searchsorted)/jit(_searchsorted_scan_impl)/vmap(jit(_searchsorted_scan_impl))/while/body/eval_jaxpr/gather | solution.py:126
  88.9 11.8 %gather_fusion = s32[2048]{0:T(1024)S(1)} fusion(s32[2048]{0:T(1024)S(1)} %get-tuple-element.368, u32[2048]{0:T(1024)S(1)} %broadcast_clamp_fusion.3), kind=kCustom, calls=%fused_computation.clone.clone.1 | custom fusion | bytes 24576 | tf_op jit(solution)/shard_map/jit(searchsorted)/jit(_searchsorted_scan_impl)/vmap(jit(_searchsorted_scan_impl))/while/body/eval_jaxpr/gather | solution.py:126
  100.8 11.8 %gather_fusion = s32[2048]{0:T(1024)S(1)} fusion(s32[2048]{0:T(1024)S(1)} %get-tuple-element.368, u32[2048]{0:T(1024)S(1)} %broadcast_clamp_fusion.3), kind=kCustom, calls=%fused_computation.clone.clone.1 | custom fusion | bytes 24576 | tf_op jit(solution)/shard_map/jit(searchsorted)/jit(_searchsorted_scan_impl)/vmap(jit(_searchsorted_scan_impl))/while/body/eval_jaxpr/gather | solution.py:126
  112.6 11.8 %gather_fusion = s32[2048]{0:T(1024)S(1)} fusion(s32[2048]{0:T(1024)S(1)} %get-tuple-element.368, u32[2048]{0:T(1024)S(1)} %broadcast_clamp_fusion.3), kind=kCustom, calls=%fused_computation.clone.clone.1 | custom fusion | bytes 24576 | tf_op jit(solution)/shard_map/jit(searchsorted)/jit(_searchsorted_scan_impl)/vmap(jit(_searchsorted_scan_impl))/while/body/eval_jaxpr/gather | solution.py:126
  124.5 11.8 %gather_fusion = s32[2048]{0:T(1024)S(1)} fusion(s32[2048]{0:T(1024)S(1)} %get-tuple-element.368, u32[2048]{0:T(1024)S(1)} %broadcast_clamp_fusion.3), kind=kCustom, calls=%fused_computation.clone.clone.1 | custom fusion | bytes 24576 | tf_op jit(solution)/shard_map/jit(searchsorted)/jit(_searchsorted_scan_impl)/vmap(jit(_searchsorted_scan_impl))/while/body/eval_jaxpr/gather | solution.py:126
  136.4 11.8 %gather_fusion = s32[2048]{0:T(1024)S(1)} fusion(s32[2048]{0:T(1024)S(1)} %get-tuple-element.368, u32[2048]{0:T(1024)S(1)} %broadcast_clamp_fusion.3), kind=kCustom, calls=%fused_computation.clone.clone.1 | custom fusion | bytes 24576 | tf_op jit(solution)/shard_map/jit(searchsorted)/jit(_searchsorted_scan_impl)/vmap(jit(_searchsorted_scan_impl))/while/body/eval_jaxpr/gather | solution.py:126
  148.2 11.8 %gather_fusion = s32[2048]{0:T(1024)S(1)} fusion(s32[2048]{0:T(1024)S(1)} %get-tuple-element.368, u32[2048]{0:T(1024)S(1)} %broadcast_clamp_fusion.3), kind=kCustom, calls=%fused_computation.clone.clone.1 | custom fusion | bytes 24576 | tf_op jit(solution)/shard_map/jit(searchsorted)/jit(_searchsorted_scan_impl)/vmap(jit(_searchsorted_scan_impl))/while/body/eval_jaxpr/gather | solution.py:126
  160.9 0.7 convert_reduce_fusion.2
  167.6 2.4 collective-permute-start.2
  170.1 2.4 collective-permute-done.2
  172.7 1.9 stack.2
  174.7 27.7 %all-to-all-start = ((bf16[512,8,384]{2,1,0:T(8,128)(2,1)}), bf16[512,8,384]{2,1,0:T(8,128)(2,1)S(1)}, u32[]{:S(2)}, u32[]{:S(2)}) async-start(bf16[512,8,384]{2,1,0:T(8,128)(2,1)} %stack.2), calls=%async_computation | async-start | bytes 6291456 | tf_op jit(solution)/shard_map/all_to_all | solution.py:129
  202.4 146.4 %all-to-all-done = bf16[512,8,384]{2,1,0:T(8,128)(2,1)S(1)} async-done(((bf16[512,8,384]{2,1,0:T(8,128)(2,1)}), bf16[512,8,384]{2,1,0:T(8,128)(2,1)S(1)}, u32[]{:S(2)}, u32[]{:S(2)}) %all-to-all-start) | async-done | bytes 3145760 | tf_op jit(solution)/shard_map/all_to_all | solution.py:129
  348.8 9.0 %gather_fusion.1 = bf16[2048,384]{1,0:T(8,128)(2,1)} fusion(bf16[4096,384]{1,0:T(8,128)(2,1)S(1)} %bitcast.82, s32[2048]{0:T(1024)S(1)} %get-tuple-element.227), kind=kCustom, calls=%fused_computation.1 | custom fusion | bytes 3153920 | tf_op jit(solution)/shard_map/jit(_take)/gather | solution.py:134
  357.8 1.6 broadcast_select_fusion
  359.5 1.4 fusion.19
  363.4 0.7 copy.50
  364.1 37.5 %while.35 = (s32[]{:T(128)}, bf16[8,8,128,128]{3,2,1,0:T(8,128)(2,1)}, bf16[8,8,128,128]{3,2,1,0:T(8,128)(2,1)}, bf16[8,8,32]{2,1,0:T(8,128)(2,1)S(1)}, bf16[128...) while((s32[]{:T(128)}, ...), condition=%wide.region_13.14_spmd, body=%wide.region_10.13_spmd.sunk | while | flops 415761408 | bytes 12229241 | solution.py:174
  364.1 1.0 constant_dynamic-slice_fusion.5
  366.6 0.7 multiply_convert_fusion.5
  367.4 0.7 fusion.93
  368.1 0.7 copy_dynamic-update-slice_fusion.2
  368.8 1.0 constant_dynamic-slice_fusion.5
  371.3 0.7 multiply_convert_fusion.5
  372.1 0.7 fusion.93
  372.8 0.7 copy_dynamic-update-slice_fusion.2
  373.5 1.0 constant_dynamic-slice_fusion.5
  376.0 0.7 multiply_convert_fusion.5
  376.7 0.7 fusion.93
  377.5 0.7 copy_dynamic-update-slice_fusion.2
  378.2 1.0 constant_dynamic-slice_fusion.5
  380.7 0.7 multiply_convert_fusion.5
  381.4 0.7 fusion.93
  382.1 0.7 copy_dynamic-update-slice_fusion.2
  382.9 1.0 constant_dynamic-slice_fusion.5
  385.4 0.7 multiply_convert_fusion.5
  386.1 0.7 fusion.93
  386.8 0.7 copy_dynamic-update-slice_fusion.2
  387.6 1.0 constant_dynamic-slice_fusion.5
  390.1 0.7 multiply_convert_fusion.5
  390.8 0.7 fusion.93
  391.5 0.7 copy_dynamic-update-slice_fusion.2
  392.3 1.0 constant_dynamic-slice_fusion.5
  394.7 0.7 multiply_convert_fusion.5
  395.5 0.7 fusion.93
  396.2 0.7 copy_dynamic-update-slice_fusion.2
  396.9 1.0 constant_dynamic-slice_fusion.5
  399.4 0.7 multiply_convert_fusion.5
  400.1 0.7 fusion.93
  400.9 0.7 copy_dynamic-update-slice_fusion.2
  (169 shorter events, 19.6 us)
Async XLA Ops:
  0.6 362.2 %copy-start = (bf16[32,32,128]{2,1,0:T(8,128)(2,1)S(1)}, bf16[32,32,128]{2,1,0:T(8,128)(2,1)}, u32[]{:S(2)}) copy-start(bf16[32,32,128]{2,1,0:T(8,128)(2,1)} %param.35) | copy-start | bytes 786436
  3.5 162.5 %collective-permute-start.1 = (bf16[64,256]{1,0:T(8,128)(2,1)S(1)}, bf16[64,256]{1,0:T(8,128)(2,1)S(1)}, u32[]{:S(2)}, u32[]{:S(2)}) collective-permute-start(bf16[64,256]{1,0:T(8,128)(2,1)S(1)} %convolution_convert_fusion.3), channel_id=1, source_target_pairs={{1,0},{2,1},{3,2},{4,3},{5,4},{6,5},{7,6},{8,7},{9,8},{10,9},{11,1... | collective-permute-start | bytes 98312 | tf_op jit(solution)/shard_map/ppermute | solution.py:22
  12.2 153.8 %collective-permute-start = (bf16[64,256]{1,0:T(8,128)(2,1)S(1)}, bf16[64,256]{1,0:T(8,128)(2,1)S(1)}, u32[]{:S(2)}, u32[]{:S(2)}) collective-permute-start(bf16[64,256]{1,0:T(8,128)(2,1)S(1)} %convolution_convert_fusion.3), channel_id=1, source_target_pairs={{0,1},{1,2},{2,3},{3,4},{4,5},{5,6},{6,7},{7,8},{8,9},{9,10},{10,1... | collective-permute-start | bytes 98312 | tf_op jit(solution)/shard_map/ppermute | solution.py:19
  17.6 143.1 %copy-start.3 = (bf16[64,128]{1,0:T(8,128)(2,1)S(1)}, bf16[64,128]{1,0:T(8,128)(2,1)}, u32[]{:S(2)}) copy-start(bf16[64,128]{1,0:T(8,128)(2,1)} %param.22) | copy-start | bytes 49156
  17.6 143.1 %copy-start.11 = (bf16[128,128]{1,0:T(8,128)(2,1)S(1)}, bf16[128,128]{1,0:T(8,128)(2,1)}, u32[]{:S(2)}) copy-start(bf16[128,128]{1,0:T(8,128)(2,1)} %param.26) | copy-start | bytes 98308
  17.6 143.1 %copy-start.12 = (f32[128]{0:T(128)S(1)}, f32[128]{0:T(128)}, u32[]{:S(2)}) copy-start(f32[128]{0:T(128)} %param.25) | copy-start | bytes 1540
  160.1 7.1 %copy-start.5 = (bf16[128,128]{1,0:T(8,128)(2,1)S(1)}, bf16[128,128]{1,0:T(8,128)(2,1)}, u32[]{:S(2)}) copy-start(bf16[128,128]{1,0:T(8,128)(2,1)} %param.29) | copy-start | bytes 98308
  160.1 7.2 %copy-start.4 = (bf16[128,384]{1,0:T(8,128)(2,1)S(1)}, bf16[128,384]{1,0:T(8,128)(2,1)}, u32[]{:S(2)}) copy-start(bf16[128,384]{1,0:T(8,128)(2,1)} %param.30) | copy-start | bytes 294916
  167.6 4.9 %collective-permute-start.2 = (f32[1,384]{1,0:T(1,128)S(1)}, f32[1,384]{1,0:T(1,128)S(1)}, u32[]{:S(2)}, u32[]{:S(2)}) collective-permute-start(f32[1,384]{1,0:T(1,128)S(1)} %fusion.38), channel_id=1, source_target_pairs={{1,0},{2,1},{3,2},{4,3},{5,4},{6,5},{7,6},{8,7},{9,8},{10,9},{11,1... | collective-permute-start | bytes 4616 | tf_op jit(solution)/shard_map/ppermute | solution.py:30
  174.7 174.1 %all-to-all-start = ((bf16[512,8,384]{2,1,0:T(8,128)(2,1)}), bf16[512,8,384]{2,1,0:T(8,128)(2,1)S(1)}, u32[]{:S(2)}, u32[]{:S(2)}) async-start(bf16[512,8,384]{2,1,0:T(8,128)(2,1)} %stack.2), calls=%async_computation | async-start | bytes 6291456 | tf_op jit(solution)/shard_map/all_to_all | solution.py:129
  357.8 1.6 copy-start.10
  357.8 3.7 copy-start.6
  359.5 2.8 copy-start.7
  362.9 1.2 copy-start.1
  362.9 1.2 copy-start.2
  362.9 1.2 copy-start.8
  362.9 1.2 copy-start.9
